TPU v7x, 32 devices: a whole 2x2x4 slice. The times are simulated.
32 devices in a mesh: ctx: 8 (over z, y), mp: 4 (over x, core).
Axes of the slice: x: 2, y: 2, z: 4, core: 2. Of those that a mesh axis runs over, the one named last changes fastest.
Arguments:
- query: bfloat16 [32, 8, 8, 128], P(('ctx', 'mp')), may hold values from -8 to 8
- keys: bfloat16 [32, 8, 2048, 128], P(('ctx', 'mp')), may hold values from -5 to 5
- values: bfloat16 [32, 8, 2048, 128], P(('ctx', 'mp')), may hold values from -6 to 6
- chosen: int32 [8, 32, 16], replicated, may hold values from 0 to 31, all different within a row; in each aligned block of 32 rows (0 to 31, 32 to 63, ..., all dimensions but the last counted through in order) at most 32 rows name the same one
- residual: bfloat16 [32, 8192], P('ctx', 'mp'), may hold values from -1.5 to 1.5
- output_weight: bfloat16 [8192, 8192], P('ctx', 'mp'), may hold values from -0.0625 to 0.0625
- norm_gain: float32 [8192], P('mp'), may hold values from 0.5 to 1.5
- gate_weight: bfloat16 [8192, 14336], P('mp', 'ctx'), may hold values from -0.0625 to 0.0625
- up_weight: bfloat16 [8192, 14336], P('mp', 'ctx'), may hold values from -0.0625 to 0.0625
- down_weight: bfloat16 [14336, 8192], P('ctx', 'mp'), may hold values from -0.046875 to 0.046875
Outputs:
- stream: bfloat16 [32, 8192], P('ctx', 'mp')
- update: bfloat16 [32, 8192], P('ctx', 'mp')
Inputs may be any that keep to these rules, and one draw needn't show every extreme that they name: `chosen`: for each KV head, each row lists 16 different partitions; no partition is listed by more than 32 rows of one KV head, and in every draw some partition is listed by exactly 32 rows of some KV head.
All inputs are finite; a program needn't handle non-finite values.
Results may differ from a plain program's by a relative error of at most 0.025.
Values may be sent and summed in bfloat16 or wider, within the bound.
No kernel may reach another device: no remote copies, remote signals or barrier semaphores. Data moves between devices by JAX's collectives and lax.ppermute only.
A program may use at most 128 MiB of HBM per device.

v0:
```python
import jax
import jax.numpy as jnp
from jax import lax
from jax.sharding import PartitionSpec as P

MODEL_WIDTH = 8192
KEPT_PARTITIONS = 16
ROW_DEV = 1
norm_eps = 1e-05
lowest_value = -1e30


def find_slots(listed, target, capacity):
    member = jnp.any(listed == target, axis=2)
    places = jnp.cumsum(member.astype(jnp.int32), axis=1) - 1
    live_count = jnp.sum(member.astype(jnp.int32), axis=1)
    slot_ranks = jnp.arange(capacity, dtype=jnp.int32)
    slot_hits = member[:, :, None] & (places[:, :, None] == slot_ranks[None, None, :])
    row_numbers = jnp.arange(listed.shape[1], dtype=jnp.int32)
    slot_rows = jnp.sum(jnp.where(slot_hits, row_numbers[None, :, None], 0), axis=1)
    slot_valid = slot_ranks[None, :] < live_count[:, None]
    return (slot_rows, slot_valid)


def global_scaling(block_max, block_sum, block_value, slot_rows, slot_valid, all_rows, head_ids):
    kv_heads, capacity, group_size = block_max.shape
    valid_wide = slot_valid[:, :, None]
    max_table = jnp.full((all_rows, kv_heads, group_size), lowest_value, jnp.float32)
    max_table = max_table.at[slot_rows, head_ids[:, None]].max(
        jnp.where(valid_wide, block_max, lowest_value)
    )
    row_top = lax.pmax(max_table.astype(jnp.bfloat16), ("ctx", "mp")).astype(max_table.dtype)
    factor = jnp.where(valid_wide, jnp.exp(block_max - row_top[slot_rows, head_ids[:, None]]), 0.0)
    return (block_value * factor[..., None], block_sum * factor)


def to_owners(array, kv_heads, capacity, per_head, ctx_count):
    shaped = array.reshape(kv_heads, capacity, per_head, -1)
    return jnp.transpose(shaped, (0, 2, 1, 3)).reshape(ctx_count, capacity, -1)


def per_device(
    query,
    keys,
    values,
    chosen,
    residual,
    output_weight,
    norm_gain,
    gate_weight,
    up_weight,
    down_weight,
):
    kv_heads = query.shape[1]
    group_size = query.shape[2]
    head_dim = query.shape[3]
    score_scale = head_dim ** (-0.5)
    ctx_count = lax.axis_size("ctx")
    mp_count = lax.axis_size("mp")
    ctx_place = lax.axis_index("ctx")
    mp_place = lax.axis_index("mp")
    own_part = ctx_place * mp_count + mp_place
    all_queries = lax.all_gather(query, ("ctx", "mp"), axis=0, tiled=True)
    all_rows = all_queries.shape[0]
    capacity = min(4 * ROW_DEV * KEPT_PARTITIONS, all_rows)
    slot_rows, slot_valid = find_slots(chosen, own_part, capacity)
    head_ids = jnp.arange(kv_heads, dtype=jnp.int32)
    picked = all_queries[slot_rows, head_ids[:, None]].reshape(
        kv_heads, capacity * group_size, head_dim
    )

    def attend(inputs):
        query_block, key_block, value_block = inputs
        scores = (
            lax.dot_general(
                query_block, key_block, (((1,), (1,)), ((), ())), preferred_element_type=jnp.float32
            )
            * score_scale
        )
        block_max = jnp.max(scores, axis=1)
        probs = jnp.exp(scores - block_max[:, None])
        block_sum = jnp.sum(probs, axis=1)
        block_value = jnp.dot(
            probs.astype(jnp.bfloat16), value_block, preferred_element_type=jnp.float32
        )
        return (block_max, block_sum, block_value)

    block_max, block_sum, block_value = lax.map(attend, (picked, keys[0], values[0]))
    block_max = block_max.reshape(kv_heads, capacity, group_size)
    block_sum = block_sum.reshape(kv_heads, capacity, group_size)
    block_value = block_value.reshape(kv_heads, capacity, group_size, head_dim)
    per_head = ctx_count // kv_heads
    feat_width = kv_heads * group_size * head_dim // ctx_count
    head_share = kv_heads * group_size // ctx_count
    own_head = ctx_place // per_head
    head_lists = lax.dynamic_index_in_dim(chosen, own_head, 0, keepdims=True)
    sources = jnp.arange(ctx_count, dtype=jnp.int32) * mp_count + mp_place
    source_rows = jax.vmap(lambda source: find_slots(head_lists, source, capacity)[0])(sources)[
        :, 0
    ]
    weighted, scaled_sum = global_scaling(
        block_max, block_sum, block_value, slot_rows, slot_valid, all_rows, head_ids
    )
    send_values = to_owners(weighted, kv_heads, capacity, per_head, ctx_count)
    send_sums = to_owners(scaled_sum, kv_heads, capacity, per_head, ctx_count)
    got_values, got_sums = (
        lax.all_to_all(
            send_values.astype(jnp.bfloat16), "ctx", split_axis=0, concat_axis=0, tiled=True
        ).astype(send_values.dtype),
        lax.all_to_all(
            send_sums.astype(jnp.bfloat16), "ctx", split_axis=0, concat_axis=0, tiled=True
        ).astype(send_sums.dtype),
    )
    numerator = jnp.zeros((all_rows, feat_width), jnp.float32).at[source_rows].add(got_values)
    denominator = jnp.zeros((all_rows, head_share), jnp.float32).at[source_rows].add(got_sums)
    numerator, denominator = (
        lax.psum(numerator.astype(jnp.bfloat16), "mp").astype(jnp.float32),
        lax.psum(denominator.astype(jnp.bfloat16), "mp").astype(jnp.float32),
    )
    attended = (
        (numerator.reshape(all_rows, -1, head_dim) / denominator[:, :, None])
        .reshape(all_rows, -1)
        .astype(jnp.bfloat16)
    )
    rows_here = attended
    projected = lax.psum_scatter(
        jnp.dot(rows_here, output_weight, preferred_element_type=jnp.float32),
        "ctx",
        scatter_dimension=0,
        tiled=True,
    )
    stream = (residual.astype(jnp.float32) + projected).astype(jnp.bfloat16)
    stream_wide = stream.astype(jnp.float32)
    squares = lax.psum(jnp.sum(stream_wide * stream_wide, axis=1), "mp")
    normed = (
        stream_wide * lax.rsqrt(squares / MODEL_WIDTH + norm_eps)[:, None] * norm_gain
    ).astype(jnp.bfloat16)
    row_piece = lax.all_gather(normed, "ctx", axis=0, tiled=True)
    gate_piece = jnp.dot(row_piece, gate_weight, preferred_element_type=jnp.float32)
    up_piece = jnp.dot(row_piece, up_weight, preferred_element_type=jnp.float32)
    gate_up = jnp.stack([gate_piece, up_piece], axis=1)
    gate_up = lax.psum(gate_up.astype(jnp.bfloat16), "mp").astype(jnp.float32)
    hidden = (jax.nn.silu(gate_up[:, 0]) * gate_up[:, 1]).astype(jnp.bfloat16)
    rows_here = hidden
    update = lax.psum_scatter(
        jnp.dot(rows_here, down_weight, preferred_element_type=jnp.float32),
        "ctx",
        scatter_dimension=0,
        tiled=True,
    ).astype(jnp.bfloat16)
    return (stream, update)


def solution(mesh):
    return jax.shard_map(
        per_device,
        mesh=mesh,
        in_specs=(
            P(("ctx", "mp"), None, None, None),
            P(("ctx", "mp"), None, None, None),
            P(("ctx", "mp"), None, None, None),
            P(),
            P("ctx", "mp"),
            P("ctx", "mp"),
            P("mp"),
            P("mp", "ctx"),
            P("mp", "ctx"),
            P("ctx", "mp"),
        ),
        out_specs=(P("ctx", "mp"), P("ctx", "mp")),
        check_vma=False,
    )
```

profile of v0, /device:TPU:0, one launch (start us, length us, event | category | flops | bytes accessed | tf_op | source)
XLA Modules:
  0.0 393.7 jit_solution(18156708375648113719)
XLA Ops:
  7.2 0.9 compare_reduce_fusion
  8.6 44.9 %all_gather.6 = bf16[32,8,8,128]{3,2,1,0:T(8,128)(2,1)S(1)} all-gather(bf16[1,8,8,128]{3,2,1,0:T(8,128)(2,1)} %param.12), channel_id=1, replica_groups=mesh['ctx'=8,'mp'=4] {'ctx','mp'}, dimensions={0}, use_global_device_ids=true | all-gather | bytes 540672 | tf_op jit(solution)/shard_map/all_gather | solution.py:63
  53.5 1.1 gather_fusion
  54.7 29.4 %while.14 = (s32[]{:T(128)}, f32[8,256]{1,0:T(8,128)S(1)}, f32[8,256]{1,0:T(8,128)S(1)}, f32[8,256,128]{2,1,0:T(8,128)S(1)}, bf16[8,256,128]{2,1,0:T(8,128)(2,1)...) while((s32[]{:T(128)}, f32[8,256]{1,0:T(8,128)S(1)}, ...), condition=%wide.region_9.10_spmd, body=%wide.region_6.9_spmd.sunk | while | flops 271580672 | bytes 7546981 | solution.py:88
  54.7 1.6 fusion.55
  56.2 1.6 fusion.57
  57.8 0.4 fusion.56
  58.3 1.6 fusion.55
  59.9 1.6 fusion.57
  62.0 1.6 fusion.55
  63.6 1.6 fusion.57
  65.7 1.6 fusion.55
  67.3 1.6 fusion.57
  69.4 1.6 fusion.55
  71.0 1.6 fusion.57
  73.1 1.6 fusion.55
  74.6 1.6 fusion.57
  76.7 1.6 fusion.55
  78.3 1.6 fusion.57
  80.4 1.6 fusion.55
  82.0 1.6 fusion.57
  84.5 12.0 %scatter_fusion = f32[32,8,8]{2,1,0:T(8,128)S(1)} fusion(f32[32,8,8]{2,1,0:T(8,128)S(1)} %broadcast_in_dim.110, s32[256]{0:T(256)S(1)} %reshape.167, f32[256,8]{1,0:T(8,128)S(1)} %bitcast.98), kind=kCustom, calls=%fused_computation.2 | custom fusion | flops 2048 | bytes 26624 | tf_op jit(solution)/shard_map/scatter-max | solution.py:29
  96.5 37.2 %pmax.7 = bf16[32,8,8]{2,1,0:T(8,128)(2,1)S(1)} all-reduce(bf16[32,8,8]{2,1,0:T(8,128)(2,1)S(1)} %convert_element_type.80), channel_id=1, replica_groups=mesh['ctx'=8,'mp'=4] {'ctx','mp'}, use_global_device_ids=true, to_apply=%region_12.13 | all-reduce | flops 2048 | bytes 8192 | tf_op jit(solution)/shard_map/pmax | solution.py:32
  133.8 1.4 gather_fusion.1
  136.0 0.9 multiply_convert_fusion
  136.9 6.1 %all-to-all-start = ((bf16[8,32,1024]{2,1,0:T(8,128)(2,1)}), bf16[8,32,1024]{2,1,0:T(8,128)(2,1)S(1)}, u32[]{:S(2)}, u32[]{:S(2)}) async-start(bf16[8,32,1024]{2,1,0:T(8,128)(2,1)} %multiply_convert_fusion), calls=%async_computation | async-start | bytes 1048576 | tf_op jit(solution)/shard_map/all_to_all | solution.py:107
  143.1 0.7 dynamic-slice_bitcast_fusion
  144.3 11.5 %all-to-all-done = bf16[8,32,1024]{2,1,0:T(8,128)(2,1)S(1)} async-done(((bf16[8,32,1024]{2,1,0:T(8,128)(2,1)}), bf16[8,32,1024]{2,1,0:T(8,128)(2,1)S(1)}, u32[]{:S(2)}, u32[]{:S(2)}) %all-to-all-start) | async-done | bytes 524320 | tf_op jit(solution)/shard_map/all_to_all | solution.py:107
  155.8 2.7 scatter_custom_fusion.1
  158.5 0.6 convert_element_type.84
  159.4 9.9 %all_to_all.10 = bf16[8,2,128]{2,1,0:T(2,128)(2,1)S(1)} all-to-all(bf16[8,2,128]{2,1,0:T(2,128)(2,1)S(1)} %reshape.200), channel_id=1, replica_groups=mesh['ctx'=8,'mp'=4] {'ctx'}, dimensions={0} | all-to-all | bytes 8192 | tf_op jit(solution)/shard_map/all_to_all | solution.py:110
  169.5 1.8 scatter_custom_fusion.2
  171.3 6.0 %psum.29 = bf16[32,8]{1,0:T(8,128)(2,1)S(1)} all-reduce(bf16[32,8]{1,0:T(8,128)(2,1)S(1)} %convert_element_type.88), channel_id=1, replica_groups=mesh['ctx'=8,'mp'=4] {'mp'}, use_global_device_ids=true, to_apply=%region_16.17 | all-reduce | flops 256 | bytes 1024 | tf_op jit(solution)/shard_map/psum | solution.py:118
  177.4 12.6 %all-reduce.7.cloned.1.call-done = bf16[32,1024]{1,0:T(8,128)(2,1)} async-done(((bf16[32,1024]{1,0:T(8,128)(2,1)}), bf16[32,1024]{1,0:T(8,128)(2,1)}) %all-reduce.7.cloned.1.call-update) | async-done | bytes 65552 | tf_op jit(solution)/shard_map/psum | solution.py:117
  190.0 3.7 fusion.25
  193.8 0.6 dynamic-slice
  195.1 69.9 %all-reduce.11.cloned.1.call-done = f32[32,2048]{1,0:T(8,128)} async-done(((f32[32,2048]{1,0:T(8,128)}), f32[32,2048]{1,0:T(8,128)}) %all-reduce.11.cloned.1.call-update) | async-done | bytes 262160
  265.0 1.0 fusion.28
  266.0 5.7 %psum.30 = f32[4]{0:T(128)S(1)} all-reduce(f32[4]{0:T(128)S(1)} %get-tuple-element.58), channel_id=1, replica_groups=mesh['ctx'=8,'mp'=4] {'mp'}, use_global_device_ids=true, to_apply=%region_19.20 | all-reduce | flops 4 | bytes 32 | tf_op jit(solution)/shard_map/psum | solution.py:134
  271.7 30.8 %all-gather = bf16[8,4,2048]{2,1,0:T(4,128)(2,1)S(1)} all-gather(bf16[1,4,2048]{2,1,0:T(4,128)(2,1)S(1)} %fusion.32), channel_id=1, replica_groups=mesh['ctx'=8,'mp'=4] {'ctx'}, dimensions={0}, use_global_device_ids=true | all-gather | bytes 147456 | tf_op jit(solution)/shard_map/all_gather | solution.py:138
  302.5 4.6 %fusion.13 = bf16[32,1,1792]{2,0,1:T(8,128)(2,1)S(1)} fusion(bf16[32,2048]{1,0:T(8,128)(2,1)S(1)} %reshape.193, bf16[2048,1792]{1,0:T(8,128)(2,1)} %param.19), kind=kOutput, calls=%fused_computation.22 | convolution fusion | flops 234938368 | bytes 7585792 | tf_op jit(solution)/shard_map/dot_general | solution.py:139
  307.1 1.3 fusion.14
  308.5 0.7 pad_maximum_fusion
  309.2 31.7 %all-reduce.9.cloned.1.call-done = bf16[32,2,1792]{2,0,1:T(8,128)(2,1)} async-done(((bf16[32,2,1792]{2,0,1:T(8,128)(2,1)}), bf16[32,2,1792]{2,0,1:T(8,128)(2,1)}) %all-reduce.9.cloned.1.call-update) | async-done | bytes 229392 | tf_op jit(solution)/shard_map/psum | solution.py:142
  340.9 1.0 convert_element_type.94
  341.9 4.4 %fusion.22 = f32[32,2048]{1,0:T(8,128)S(1)} fusion(bf16[1792,2048]{1,0:T(8,128)(2,1)} %param.21, f32[32,2,1792]{2,0,1:T(8,128)S(1)} %convert_element_type.94), kind=kOutput, calls=%fused_computation.42 | convolution fusion | flops 235225088 | bytes 8060928 | tf_op jit(solution)/shard_map/dot_general | solution.py:146
  346.3 40.2 %all-reduce.12 = bf16[32,2048]{1,0:T(8,128)(2,1)S(1)} all-reduce(f32[32,2048]{1,0:T(8,128)S(1)} %fusion.22), channel_id=3, replica_groups=mesh['ctx'=8,'mp'=4] {'ctx'}, use_global_device_ids=true, to_apply=%region_21.22.clone | all-reduce | flops 65536 | bytes 393216
  386.5 0.6 dynamic-slice_convert_fusion
  (81 shorter events, 6.8 us)
Async XLA Ops:
  136.9 56.9 %copy-start.3 = (u32[32]{0:T(128)S(1)}, u32[32]{0:T(128)}, u32[]{:S(2)}) copy-start(u32[32]{0:T(128)} %constant.135) | copy-start | bytes 388
  136.9 128.0 %copy-start.1 = (bf16[4,2048]{1,0:T(4,128)(2,1)S(1)}, bf16[4,2048]{1,0:T(4,128)(2,1)}, u32[]{:S(2)}) copy-start(bf16[4,2048]{1,0:T(4,128)(2,1)} %param.16) | copy-start | bytes 49156
  136.9 134.7 %copy-start.2 = (f32[2048]{0:T(1024)S(1)}, f32[2048]{0:T(1024)}, u32[]{:S(2)}) copy-start(f32[2048]{0:T(1024)} %param.18) | copy-start | bytes 24580
  136.9 18.8 %all-to-all-start = ((bf16[8,32,1024]{2,1,0:T(8,128)(2,1)}), bf16[8,32,1024]{2,1,0:T(8,128)(2,1)S(1)}, u32[]{:S(2)}, u32[]{:S(2)}) async-start(bf16[8,32,1024]{2,1,0:T(8,128)(2,1)} %multiply_convert_fusion), calls=%async_computation | async-start | bytes 1048576 | tf_op jit(solution)/shard_map/all_to_all | solution.py:107
  143.0 46.9 %all-reduce.7.cloned.1.call-start = ((), (), s32[]{:S(2)}) async-start(), calls=%async_computation.2 | async-start | bytes 131072 | tf_op jit(solution)/shard_map/psum | solution.py:117
  159.2 105.8 %all-reduce.11.cloned.1.call-start = ((), (), s32[]{:S(2)}) async-start(), calls=%async_computation.4 | async-start | bytes 524288
  171.3 135.8 %slice-start = ((s8[7340032]{0:T(1024)(128)(4,1)}), s8[3145728]{0:T(1024)(128)(4,1)S(1)}, s32[]{:S(2)}) async-start(s8[7340032]{0:T(1024)(128)(4,1)} %bitcast.92), calls=%async_computation.5 | async-start | bytes 6291456
  193.8 147.1 %all-reduce.9.cloned.1.call-start = ((), (), s32[]{:S(2)}) async-start(), calls=%async_computation.3 | async-start | bytes 458752 | tf_op jit(solution)/shard_map/psum | solution.py:142
  266.0 42.5 %copy-start = (bf16[4,2048]{1,0:T(4,128)(2,1)}, bf16[4,2048]{1,0:T(4,128)(2,1)S(1)}, u32[]{:S(2)}) copy-start(bf16[4,2048]{1,0:T(4,128)(2,1)S(1)} %get-tuple-element.59) | copy-start | bytes 49156
  302.5 4.6 %slice-start.1 = ((s8[7340032]{0:T(1024)(128)(4,1)}), s8[4194304]{0:T(1024)(128)(4,1)S(1)}, s32[]{:S(2)}) async-start(s8[7340032]{0:T(1024)(128)(4,1)} %bitcast.92), calls=%async_computation.6 | async-start | bytes 8388608
Sparse Core Ops, SparseCore 0:
  159.3 30.5 all-reduce.6
  193.9 71.0 all-reduce.10
  309.3 31.5 all-reduce.8
where the time goes:
time: 395 us; the launch traced here: 394 us
  blocking collectives  175 us (44%)
  waiting for transfers between devices  126 us (32%)
  matrix products  39.2 us (10%)
  other arithmetic  26.3 us (7%)
  between operations  14.7 us (4%)
  local copies, waits for them, and re-layouts  6.66 us (2%)
  starting transfers between devices  6.18 us (2%)
    unnamed x4, waiting for transfers between devices  69.9 us
    all_gather x1, blocking collectives, per_device(): all_queries = lax.all_gather(query, ('ctx', 'mp'), axis=0, tiled=True)  44.9 us
    unnamed x1, blocking collectives  40.2 us
    pmax x1, blocking collectives, global_scaling(): lax.pmax(max_table.astype(jnp.bfloat16), ('ctx', 'mp'))  37.2 us
    psum x1, waiting for transfers between devices, per_device(): gate_up = lax.psum(gate_up.astype(jnp.bfloat16), 'mp').astype(jnp.float32)  31.7 us
    all_gather x1, blocking collectives, per_device(): row_piece = lax.all_gather(normed, 'ctx', axis=0, tiled=True)  30.8 us
    dot_general x8, matrix products, attend(): jnp.dot(probs.astype(jnp.bfloat16), value_block, preferred_element_type=j...  12.6 us
    psum x1, waiting for transfers between devices, per_device(): lax.psum(numerator.astype(jnp.bfloat16), 'mp').astype(jnp.float32)  12.6 us
  transfers between devices with their start and end apart: 4, of which 4 were waited for; matrix products, arithmetic and copies ran while one was open for 1% of the time, Pallas kernels for 0%

commit v1 on v0

--- a/solution.py
+++ b/solution.py
@@ -139,7 +139,9 @@
     gate_piece = jnp.dot(row_piece, gate_weight, preferred_element_type=jnp.float32)
     up_piece = jnp.dot(row_piece, up_weight, preferred_element_type=jnp.float32)
     gate_up = jnp.stack([gate_piece, up_piece], axis=1)
-    gate_up = lax.psum(gate_up.astype(jnp.bfloat16), "mp").astype(jnp.float32)
+    gate_up = jnp.sum(lax.all_gather(gate_up.astype(jnp.bfloat16), "mp"), axis=0).astype(
+        jnp.float32
+    )
     hidden = (jax.nn.silu(gate_up[:, 0]) * gate_up[:, 1]).astype(jnp.bfloat16)
     rows_here = hidden
     update = lax.psum_scatter(

time: 395 us -> 370 us (0.937)
  waiting for transfers between devices: 126 us -> 94 us
  blocking collectives: 175 us -> 182 us
    psum x1 -> x0, waiting for transfers between devices: 31.7 us -> none  [per_device(): gate_up = lax.psum(gate_up.astype(jnp.bfloat16), 'mp').astype(jnp.float32)]
    all_gather x0 -> x1, blocking collectives: none -> 9.5 us  [per_device(): lax.all_gather(gate_up.astype(jnp.bfloat16), 'mp')]
    unnamed x4 -> x3, waiting for transfers between devices: 69.9 us -> 70 us
  transfers between devices with their start and end apart: 4 -> 3, of which waited for: 4 -> 3; matrix products, arithmetic and copies ran while one was open for 1% -> 1% of each run, Pallas kernels for 0% -> 0%
where the time goes in v1:
time: 370 us; the launch traced here: 369 us
  blocking collectives  182 us (49%)
  waiting for transfers between devices  94 us (25%)
  matrix products  39.1 us (11%)
  other arithmetic  24.8 us (7%)
  between operations  15 us (4%)
  local copies, waits for them, and re-layouts  6.66 us (2%)
  starting transfers between devices  6.13 us (2%)
    unnamed x3, waiting for transfers between devices  70 us
    all_gather x1, blocking collectives, per_device(): all_queries = lax.all_gather(query, ('ctx', 'mp'), axis=0, tiled=True)  44.9 us
    unnamed x1, blocking collectives  38.4 us
    pmax x1, blocking collectives, global_scaling(): lax.pmax(max_table.astype(jnp.bfloat16), ('ctx', 'mp'))  37.2 us
    all_gather x1, blocking collectives, per_device(): row_piece = lax.all_gather(normed, 'ctx', axis=0, tiled=True)  30.8 us
    dot_general x8, matrix products, attend(): jnp.dot(probs.astype(jnp.bfloat16), value_block, preferred_element_type=j...  12.6 us
    psum x1, waiting for transfers between devices, per_device(): lax.psum(numerator.astype(jnp.bfloat16), 'mp').astype(jnp.float32)  12.6 us
    dot_general x8, matrix products, attend(): lax.dot_general(query_block, key_block, (((1,), (1,)), ((), ())), preferr...  12.5 us
  transfers between devices with their start and end apart: 3, of which 3 were waited for; matrix products, arithmetic and copies ran while one was open for 1% of the time, Pallas kernels for 0%

profile of v1, /device:TPU:0, one launch (start us, length us, event | category | flops | bytes accessed | tf_op | source)
XLA Modules:
  0.0 368.6 jit_solution(12747950885445134333)
XLA Ops:
  7.2 0.9 compare_reduce_fusion
  8.6 44.9 %all_gather.10 = bf16[32,8,8,128]{3,2,1,0:T(8,128)(2,1)S(1)} all-gather(bf16[1,8,8,128]{3,2,1,0:T(8,128)(2,1)} %param.12), channel_id=1, replica_groups=mesh['ctx'=8,'mp'=4] {'ctx','mp'}, dimensions={0}, use_global_device_ids=true | all-gather | bytes 540672 | tf_op jit(solution)/shard_map/all_gather | solution.py:63
  53.5 1.1 gather_fusion
  54.7 29.4 %while.14 = (s32[]{:T(128)}, f32[8,256]{1,0:T(8,128)S(1)}, f32[8,256]{1,0:T(8,128)S(1)}, f32[8,256,128]{2,1,0:T(8,128)S(1)}, bf16[8,256,128]{2,1,0:T(8,128)(2,1)...) while((s32[]{:T(128)}, f32[8,256]{1,0:T(8,128)S(1)}, ...), condition=%wide.region_9.10_spmd, body=%wide.region_6.9_spmd.sunk | while | flops 271580672 | bytes 7546981 | solution.py:88
  54.7 1.6 fusion.55
  56.2 1.6 fusion.57
  57.8 0.4 fusion.56
  58.3 1.6 fusion.55
  59.9 1.6 fusion.57
  61.5 0.4 fusion.56
  62.0 1.6 fusion.55
  63.6 1.6 fusion.57
  65.2 0.4 fusion.56
  65.7 1.6 fusion.55
  67.3 1.6 fusion.57
  69.4 1.6 fusion.55
  71.0 1.6 fusion.57
  73.1 1.6 fusion.55
  74.6 1.6 fusion.57
  76.7 1.6 fusion.55
  78.3 1.6 fusion.57
  80.4 1.6 fusion.55
  82.0 1.6 fusion.57
  84.5 12.0 %scatter_fusion = f32[32,8,8]{2,1,0:T(8,128)S(1)} fusion(f32[32,8,8]{2,1,0:T(8,128)S(1)} %broadcast_in_dim.110, s32[256]{0:T(256)S(1)} %reshape.200, f32[256,8]{1,0:T(8,128)S(1)} %bitcast.98), kind=kCustom, calls=%fused_computation.2 | custom fusion | flops 2048 | bytes 26624 | tf_op jit(solution)/shard_map/scatter-max | solution.py:29
  96.5 37.2 %pmax.7 = bf16[32,8,8]{2,1,0:T(8,128)(2,1)S(1)} all-reduce(bf16[32,8,8]{2,1,0:T(8,128)(2,1)S(1)} %convert_element_type.89), channel_id=1, replica_groups=mesh['ctx'=8,'mp'=4] {'ctx','mp'}, use_global_device_ids=true, to_apply=%region_12.13 | all-reduce | flops 2048 | bytes 8192 | tf_op jit(solution)/shard_map/pmax | solution.py:32
  133.8 1.4 gather_fusion.1
  136.0 0.9 multiply_convert_fusion
  137.0 6.1 %all-to-all-start = ((bf16[8,32,1024]{2,1,0:T(8,128)(2,1)}), bf16[8,32,1024]{2,1,0:T(8,128)(2,1)S(1)}, u32[]{:S(2)}, u32[]{:S(2)}) async-start(bf16[8,32,1024]{2,1,0:T(8,128)(2,1)} %multiply_convert_fusion), calls=%async_computation | async-start | bytes 1048576 | tf_op jit(solution)/shard_map/all_to_all | solution.py:107
  143.1 0.7 dynamic-slice_bitcast_fusion
  144.3 11.5 %all-to-all-done = bf16[8,32,1024]{2,1,0:T(8,128)(2,1)S(1)} async-done(((bf16[8,32,1024]{2,1,0:T(8,128)(2,1)}), bf16[8,32,1024]{2,1,0:T(8,128)(2,1)S(1)}, u32[]{:S(2)}, u32[]{:S(2)}) %all-to-all-start) | async-done | bytes 524320 | tf_op jit(solution)/shard_map/all_to_all | solution.py:107
  155.8 2.7 scatter_custom_fusion.1
  158.5 0.6 convert_element_type.93
  159.4 9.9 %all_to_all.10 = bf16[8,2,128]{2,1,0:T(2,128)(2,1)S(1)} all-to-all(bf16[8,2,128]{2,1,0:T(2,128)(2,1)S(1)} %reshape.233), channel_id=1, replica_groups=mesh['ctx'=8,'mp'=4] {'ctx'}, dimensions={0} | all-to-all | bytes 8192 | tf_op jit(solution)/shard_map/all_to_all | solution.py:110
  169.5 1.8 scatter_custom_fusion.2
  171.3 6.0 %psum.22 = bf16[32,8]{1,0:T(8,128)(2,1)S(1)} all-reduce(bf16[32,8]{1,0:T(8,128)(2,1)S(1)} %convert_element_type.97), channel_id=1, replica_groups=mesh['ctx'=8,'mp'=4] {'mp'}, use_global_device_ids=true, to_apply=%region_16.17 | all-reduce | flops 256 | bytes 1024 | tf_op jit(solution)/shard_map/psum | solution.py:118
  177.4 12.6 %all-reduce.6.cloned.1.call-done = bf16[32,1024]{1,0:T(8,128)(2,1)} async-done(((bf16[32,1024]{1,0:T(8,128)(2,1)}), bf16[32,1024]{1,0:T(8,128)(2,1)}) %all-reduce.6.cloned.1.call-update) | async-done | bytes 65552 | tf_op jit(solution)/shard_map/psum | solution.py:117
  190.0 3.7 %fusion.25 = f32[32,2048]{1,0:T(8,128)} fusion(bf16[1024,2048]{1,0:T(8,128)(2,1)} %param.17, f32[4,8,8,128]{3,2,1,0:T(8,128)S(1)} %bitcast.99, bf16[32,1024]{1,0:T(8,128)(2,1)} %all-reduce.6.cloned.1.call-done), kind=kOutput, calls=%fused_computation.44 | convolution fusion | flops 134316032 | bytes 4653056 | tf_op jit(solution)/shard_map/dot_general | solution.py:127
  193.8 0.6 dynamic-slice
  195.0 69.9 %all-reduce.8.cloned.1.call-done = f32[32,2048]{1,0:T(8,128)} async-done(((f32[32,2048]{1,0:T(8,128)}), f32[32,2048]{1,0:T(8,128)}) %all-reduce.8.cloned.1.call-update) | async-done | bytes 262160
  265.0 1.0 fusion.28
  266.0 5.7 %psum.23 = f32[4]{0:T(128)S(1)} all-reduce(f32[4]{0:T(128)S(1)} %get-tuple-element.58), channel_id=1, replica_groups=mesh['ctx'=8,'mp'=4] {'mp'}, use_global_device_ids=true, to_apply=%region_19.20 | all-reduce | flops 4 | bytes 32 | tf_op jit(solution)/shard_map/psum | solution.py:134
  271.7 30.8 %all-gather = bf16[8,4,2048]{2,1,0:T(4,128)(2,1)S(1)} all-gather(bf16[1,4,2048]{2,1,0:T(4,128)(2,1)S(1)} %fusion.32), channel_id=1, replica_groups=mesh['ctx'=8,'mp'=4] {'ctx'}, dimensions={0}, use_global_device_ids=true | all-gather | bytes 147456 | tf_op jit(solution)/shard_map/all_gather | solution.py:138
  302.5 4.6 %fusion.13 = bf16[1,32,1,1792]{3,1,2,0:T(8,128)(2,1)S(1)} fusion(bf16[32,2048]{1,0:T(8,128)(2,1)S(1)} %reshape.226, bf16[2048,1792]{1,0:T(8,128)(2,1)} %param.19), kind=kOutput, calls=%fused_computation.22 | convolution fusion | flops 234938368 | bytes 7585792 | tf_op jit(solution)/shard_map/dot_general | solution.py:139
  307.1 1.3 fusion.14
  308.5 9.5 %all_gather.12 = bf16[4,32,2,1792]{3,1,2,0:T(8,128)(2,1)S(1)} all-gather(bf16[1,32,2,1792]{3,1,2,0:T(8,128)(2,1)S(1)} %pad_maximum_fusion), channel_id=1, replica_groups=mesh['ctx'=8,'mp'=4] {'mp'}, dimensions={0}, use_global_device_ids=true | all-gather | bytes 1146880 | tf_op jit(solution)/shard_map/all_gather | solution.py:142
  318.2 4.4 %fusion.22 = f32[32,2048]{1,0:T(8,128)S(1)} fusion(bf16[1792,2048]{1,0:T(8,128)(2,1)} %param.21, f32[32,2,1792]{2,0,1:T(8,128)S(1)} %convert_element_type.103), kind=kOutput, calls=%fused_computation.42 | convolution fusion | flops 235225088 | bytes 8060928 | tf_op jit(solution)/shard_map/dot_general | solution.py:148
  322.6 38.4 %all-reduce.9 = bf16[32,2048]{1,0:T(8,128)(2,1)S(1)} all-reduce(f32[32,2048]{1,0:T(8,128)S(1)} %fusion.22), channel_id=3, replica_groups=mesh['ctx'=8,'mp'=4] {'ctx'}, use_global_device_ids=true, to_apply=%region_21.22.clone | all-reduce | flops 65536 | bytes 393216
  361.1 0.6 dynamic-slice_convert_fusion
  (80 shorter events, 6.1 us)
Async XLA Ops:
  136.9 56.8 %copy-start.3 = (u32[32]{0:T(128)S(1)}, u32[32]{0:T(128)}, u32[]{:S(2)}) copy-start(u32[32]{0:T(128)} %constant.137) | copy-start | bytes 388
  136.9 128.0 %copy-start.1 = (bf16[4,2048]{1,0:T(4,128)(2,1)S(1)}, bf16[4,2048]{1,0:T(4,128)(2,1)}, u32[]{:S(2)}) copy-start(bf16[4,2048]{1,0:T(4,128)(2,1)} %param.16) | copy-start | bytes 49156
  137.0 134.7 %copy-start.2 = (f32[2048]{0:T(1024)S(1)}, f32[2048]{0:T(1024)}, u32[]{:S(2)}) copy-start(f32[2048]{0:T(1024)} %param.18) | copy-start | bytes 24580
  137.0 18.8 %all-to-all-start = ((bf16[8,32,1024]{2,1,0:T(8,128)(2,1)}), bf16[8,32,1024]{2,1,0:T(8,128)(2,1)S(1)}, u32[]{:S(2)}, u32[]{:S(2)}) async-start(bf16[8,32,1024]{2,1,0:T(8,128)(2,1)} %multiply_convert_fusion), calls=%async_computation | async-start | bytes 1048576 | tf_op jit(solution)/shard_map/all_to_all | solution.py:107
  143.0 46.9 %all-reduce.6.cloned.1.call-start = ((), (), s32[]{:S(2)}) async-start(), calls=%async_computation.2 | async-start | bytes 131072 | tf_op jit(solution)/shard_map/psum | solution.py:117
  159.2 105.8 %all-reduce.8.cloned.1.call-start = ((), (), s32[]{:S(2)}) async-start(), calls=%async_computation.3 | async-start | bytes 524288
  171.3 135.8 %slice-start = ((s8[7340032]{0:T(1024)(128)(4,1)}), s8[3145728]{0:T(1024)(128)(4,1)S(1)}, s32[]{:S(2)}) async-start(s8[7340032]{0:T(1024)(128)(4,1)} %bitcast.92), calls=%async_computation.4 | async-start | bytes 6291456
  265.9 42.5 %copy-start = (bf16[4,2048]{1,0:T(4,128)(2,1)}, bf16[4,2048]{1,0:T(4,128)(2,1)S(1)}, u32[]{:S(2)}) copy-start(bf16[4,2048]{1,0:T(4,128)(2,1)S(1)} %get-tuple-element.59) | copy-start | bytes 49156
  302.5 4.6 %slice-start.1 = ((s8[7340032]{0:T(1024)(128)(4,1)}), s8[4194304]{0:T(1024)(128)(4,1)S(1)}, s32[]{:S(2)}) async-start(s8[7340032]{0:T(1024)(128)(4,1)} %bitcast.92), calls=%async_computation.5 | async-start | bytes 8388608
Sparse Core Ops, SparseCore 0:
  159.3 30.5 all-reduce.5
  193.9 71.0 all-reduce.7
